TPU v7x, 128 devices: a whole 4x4x4 slice. The times are simulated.
128 devices in a mesh: gx: 16 (over x, z), gy: 8 (over y, core).
Axes of the slice: x: 4, y: 4, z: 4, core: 2. Of those that a mesh axis runs over, the one named last changes fastest.
Arguments:
- control: float32 [2, 32, 512, 2048], P(None, None, 'gx', 'gy'), may hold values from -6 to 6
- band_roots: float32 [16, 32, 32], replicated, may hold values from -1 to 1
Outputs:
- increment: float32 [2, 32, 512, 2048], P(None, None, 'gx', 'gy')
All inputs are finite; a program needn't handle non-finite values.
Results may differ from a plain program's by a relative error of at most 0.000053.
Values sent between devices are 32-bit elements; how exact they have to be, the bound alone decides.
A program may use at most 64 MiB of HBM per device.

v0:
```python
from functools import partial

import jax
import jax.numpy as jnp
from jax import lax
from jax.experimental import pallas as pl
from jax.experimental.pallas import tpu as pltpu
from jax.sharding import PartitionSpec as P

LEVELS = 5
F32 = jnp.float32
BF16 = jnp.bfloat16


def round_up(value, step):
    return (value + step - 1) // step * step


class Level:
    def __init__(self, planes, rows):
        self.n = planes
        self.y = rows
        self.h = planes // 2
        self.hy = rows // 2
        self.r = round_up(rows + 16, 16)
        self.rb = round_up(self.hy + 16, 16)
        self.npad = max(planes, 8)
        self.short = planes < 3
        self.sent = self.npad + 16
        self.got = self.npad + 24


def levels_of(planes, rows):
    return [Level(planes >> k, rows >> k) for k in range(LEVELS)]


def each(count, body, unroll_to=4):
    if count <= unroll_to:
        for i in range(count):
            body(i)
    else:

        @pl.loop(0, count)
        def _(i):
            body(i)


def kernel(levels, counts, x_hbm, w_ref, out_ref, *scratch):
    count_x, count_y = counts
    (xin, mats, in_sem, send_sem, recv_sem) = scratch[:5]
    per = scratch[5:]
    width = 11
    lv_refs = [per[k * width : (k + 1) * width] for k in range(LEVELS)]
    gx = lax.axis_index("gx")
    gy = lax.axis_index("gy")
    first_x, last_x = gx == 0, gx == count_x - 1
    planes_in = levels[0].n
    rows_in = levels[0].y
    cells = xin.shape[1] // planes_in

    def at(dx, dy):
        return {
            "gx": lax.rem(gx + dx + count_x, count_x),
            "gy": lax.rem(gy + dy + count_y, count_y),
        }

    friends = [
        (dx, dy) for dx in (-2, -1, 0, 1, 2) for dy in (-1, 0, 1) if (dx, dy) != (0, 0)
    ]
    barrier = pltpu.get_barrier_semaphore()
    for dx, dy in friends:
        pl.semaphore_signal(
            barrier, inc=1, device_id=at(dx, dy), device_id_type=pl.DeviceIdType.MESH
        )

    loads = [
        pltpu.make_async_copy(
            x_hbm.at[:, side * rows_in : (side + 1) * rows_in], xin.at[side], in_sem.at[side]
        )
        for side in range(2)
    ]
    for load in loads:
        load.start()

    lane = lax.broadcasted_iota(jnp.int32, (1, 128), 1)
    upper = lane >= 64
    keep_next = jnp.logical_or(lane < 64, gy < count_y - 1)
    keep_prev = jnp.logical_or(lane >= 64, gy > 0)

    block_row = lax.broadcasted_iota(jnp.int32, (128, 128), 0) // 32
    block_lane = lax.broadcasted_iota(jnp.int32, (128, 128), 1) // 32
    diagonal = block_row == block_lane

    def build(band):
        small = jnp.concatenate([w_ref[band]] * 4, axis=1)
        tiled = jnp.concatenate([small] * 4, axis=0)
        square = jnp.where(diagonal, tiled, 0.0).T
        high = square.astype(BF16)
        low = (square - high.astype(F32)).astype(BF16)
        mats[band, 0:128, 0:128] = high
        mats[band, 128:256, 0:128] = high
        mats[band, 0:128, 128:256] = low
        mats[band, 128:256, 128:256] = jnp.zeros((128, 128), BF16)

    each(16, build)

    for load in loads:
        load.wait()

    def take(x):
        low = xin[0, pl.ds(x, cells, stride=planes_in), :]
        high = xin[1, pl.ds(x, cells, stride=planes_in), :]
        tile = jnp.concatenate([low, high], axis=0)
        lv_refs[0][0][x + 1, 8 : 8 + rows_in, :] = tile.T

    each(planes_in, take)

    pl.semaphore_wait(barrier, len(friends))

    def copies(k):
        lv = levels[k]
        a, sp, en, es, rn, rs = lv_refs[k][:6]
        rows = pl.ds(8, lv.y)
        moves = [
            (a.at[1, rows], a.at[lv.n + 1, rows], (-1, 0)),
            (a.at[2, rows] if lv.short else sp.at[0], a.at[lv.n + 2, rows], (-1, 0)),
            (sp.at[1], a.at[0, rows], (1, 0)),
        ]
        if lv.short:
            moves.append((a.at[1, rows], a.at[lv.n + 3, rows], (-2, 0)))
        groups = [
            (pl.ds(0, lv.npad), pl.ds(0, lv.npad), 0),
            (pl.ds(lv.npad, 8), pl.ds(lv.npad, 8), -1),
            (pl.ds(lv.npad + 8, 8), pl.ds(lv.npad + 8, 8), 1),
        ]
        if lv.short:
            groups.append((pl.ds(lv.npad, 8), pl.ds(lv.npad + 16, 8), -2))
        for source, target, dx in groups:
            moves.append((en.at[:, source], rn.at[:, target], (dx, -1)))
            moves.append((es.at[:, source], rs.at[:, target], (dx, 1)))
        return [
            pltpu.make_async_remote_copy(
                src_ref=source,
                dst_ref=target,
                send_sem=send_sem.at[k, m],
                recv_sem=recv_sem.at[k, m],
                device_id=at(*way),
                device_id_type=pl.DeviceIdType.MESH,
            )
            for m, (source, target, way) in enumerate(moves)
        ]

    def send(k):
        lv = levels[k]
        a, sp, en, es = lv_refs[k][:4]
        n, y = lv.n, lv.y
        todo = copies(k)
        rows = pl.ds(8, y)
        if not lv.short:
            sp[0] = a[2, rows] - 0.5 * (a[1, rows] + a[3, rows])
        sp[1] = a[n, rows] - 0.5 * a[n - 1, rows]
        x_moves = 4 if lv.short else 3
        for copy in todo[:x_moves]:
            copy.start()

        def edge(x):
            one = pl.ds(x, 1)
            r0, r1, r2 = a[x + 1, 8:9], a[x + 1, 9:10], a[x + 1, 10:11]
            before, end = a[x + 1, y + 6 : y + 7], a[x + 1, y + 7 : y + 8]
            en[0, one] = r0
            en[1, one] = r1 - 0.5 * (r0 + r2)
            es[0, one] = end - 0.5 * before

        each(n, edge, 8)
        for ref, kinds in ((en, 2), (es, 1)):
            for kind in range(kinds):
                row = lambda i: ref[kind, i : i + 1]
                ref[kind, lv.npad : lv.npad + 1] = row(0)
                second = row(1) if lv.short else row(1) - 0.5 * (row(0) + row(2))
                ref[kind, lv.npad + 1 : lv.npad + 2] = second
                ref[kind, lv.npad + 8 : lv.npad + 9] = row(n - 1) - 0.5 * row(n - 2)
        for copy in todo[x_moves:]:
            copy.start()

    def receive(k):
        for copy in copies(k):
            copy.wait_recv()

    def fill(k):
        lv = levels[k]
        a, sp, en, es, rn, rs = lv_refs[k][:6]
        n, y = lv.n, lv.y

        def place(plane, f_here, d_here, q_here, slot):
            f_there, d_there, q_there = rn[0, slot], rn[1, slot], rs[0, slot]
            turn = lambda value: pltpu.roll(value, 64, 1)
            a[plane, y + 8 : y + 9] = jnp.where(
                keep_next, turn(jnp.where(upper, f_here, f_there)), 0.0
            )
            a[plane, y + 9 : y + 10] = jnp.where(
                keep_next, turn(jnp.where(upper, d_here, d_there)), 0.0
            )
            a[plane, 7:8] = turn(jnp.where(upper, q_there, q_here))

        def local(x):
            one = pl.ds(x, 1)
            place(x + 1, en[0, one], en[1, one], es[0, one], one)

        each(n, local, 8)
        halo = [(n + 1, lv.npad), (n + 2, lv.npad + 1), (0, lv.npad + 8)]
        if lv.short:
            halo.append((n + 3, lv.npad + 16))
        for plane, slot in halo:
            r0, r1, r2 = a[plane, 8:9], a[plane, 9:10], a[plane, 10:11]
            before, end = a[plane, y + 6 : y + 7], a[plane, y + 7 : y + 8]
            place(plane, r0, r1 - 0.5 * (r0 + r2), end - 0.5 * before, pl.ds(slot, 1))
        if lv.short:

            @pl.when(gx == count_x - 2)
            def _():
                a[n + 3] = jnp.zeros_like(a[n + 3])

            a[n + 2] = a[n + 2] - 0.5 * (a[n + 1] + a[n + 3])

        @pl.when(last_x)
        def _():
            a[n + 1] = jnp.zeros_like(a[n + 1])
            a[n + 2] = jnp.zeros_like(a[n + 2])

        @pl.when(first_x)
        def _():
            a[0] = 0.5 * a[1]

    def lift_x(k):
        lv = levels[k]
        a, sx, dx = lv_refs[k][0], lv_refs[k][6], lv_refs[k][7]
        n, h = lv.n, lv.h
        dx[0] = a[0] - 0.5 * a[1]

        def step(i):
            even = a[2 * i + 1]
            detail = a[2 * i + 2] - 0.5 * (even + a[2 * i + 3])
            dx[i + 1] = detail
            sx[i] = even + 0.25 * (dx[i] + detail)

        each(h, step)
        dx[h + 1] = a[n + 2]
        sx[h] = a[n + 1] + 0.25 * (dx[h] + dx[h + 1])

    def lift_y(lv, plane, smooth, detail):
        hy, y = lv.hy, lv.y
        even = plane[pl.ds(8, hy, stride=2), :]
        odd = plane[pl.ds(9, hy, stride=2), :]
        after = plane[pl.ds(10, hy, stride=2), :]
        fresh = odd - 0.5 * (even + after)
        detail[8 : 8 + hy] = fresh
        detail[7:8] = jnp.where(keep_prev, plane[7:8] - 0.5 * plane[8:9], 0.0)
        detail[8 + hy : 9 + hy] = plane[y + 9 : y + 10]
        if smooth is None:
            return
        smooth[8 : 8 + hy] = even + 0.25 * (detail[7 : 7 + hy] + fresh)
        smooth[8 + hy : 9 + hy] = plane[y + 8 : y + 9] + 0.25 * (
            detail[7 + hy : 8 + hy] + detail[8 + hy : 9 + hy]
        )

    def lift_smooth(k):
        lv = levels[k]
        sx, b0 = lv_refs[k][6], lv_refs[k][8]
        coarse = lv_refs[k + 1][0] if k + 1 < LEVELS else None
        if coarse is None:
            target = mats_s5

            def step(i):
                lift_y(lv, sx.at[i], target.at[i], b0.at[i])

            each(lv.h + 1, step)
        else:

            def step(i):
                lift_y(lv, sx.at[i], coarse.at[i + 1], b0.at[i])

            each(lv.h, step)
            lift_y(lv, sx.at[lv.h], None, b0.at[lv.h])

    def lift_detail(k):
        lv = levels[k]
        dx, b1, b2 = lv_refs[k][7], lv_refs[k][9], lv_refs[k][10]

        def step(i):
            lift_y(lv, dx.at[i], b1.at[i], b2.at[i])

        each(lv.h + 2, step)

    def weigh(ref, i, band):
        value = ref[i]
        high = value.astype(BF16)
        low = (value - high.astype(F32)).astype(BF16)
        both = jnp.concatenate([high, low], axis=1)
        product = jnp.dot(both, mats[band], preferred_element_type=F32)
        ref[i] = product[:, :128] + product[:, 128:]

    def weigh_bands(k):
        lv = levels[k]
        b0, b1, b2 = lv_refs[k][8:11]
        each(lv.h + 1, lambda i: weigh(b0, i, 3 * k))
        each(lv.h + 2, lambda i: weigh(b1, i, 3 * k + 1))
        each(lv.h + 2, lambda i: weigh(b2, i, 3 * k + 2))

    def unlift_y(lv, smooth, detail, plane):
        hy, y = lv.hy, lv.y
        fresh = detail[8 : 8 + hy]
        even = smooth[8 : 8 + hy] - 0.25 * (detail[7 : 7 + hy] + fresh)
        plane[pl.ds(8, hy, stride=2), :] = even
        last = smooth[8 + hy : 9 + hy] - 0.25 * (
            detail[7 + hy : 8 + hy] + detail[8 + hy : 9 + hy]
        )
        plane[y + 8 : y + 9] = jnp.where(keep_next, last, 0.0)
        after = plane[pl.ds(10, hy, stride=2), :]
        plane[pl.ds(9, hy, stride=2), :] = fresh + 0.5 * (even + after)

    def unlift_detail(k):
        lv = levels[k]
        dx, b1, b2 = lv_refs[k][7], lv_refs[k][9], lv_refs[k][10]
        each(lv.h + 2, lambda i: unlift_y(lv, b1.at[i], b2.at[i], dx.at[i]))

    def unlift_smooth(k, coarse):
        lv = levels[k]
        sx, b0 = lv_refs[k][6], lv_refs[k][8]
        shift = 0 if k + 1 == LEVELS else 1
        each(
            lv.h + 1, lambda i: unlift_y(lv, coarse.at[i + shift], b0.at[i], sx.at[i])
        )

    def unlift_x(k, target, emit=None):
        lv = levels[k]
        sx, dx = lv_refs[k][6], lv_refs[k][7]
        n, h = lv.n, lv.h
        target[1] = sx[0] - 0.25 * (dx[0] + dx[1])

        @pl.when(jnp.logical_not(last_x))
        def _():
            target[n + 1] = sx[h] - 0.25 * (dx[h] + dx[h + 1])

        @pl.when(last_x)
        def _():
            target[n + 1] = jnp.zeros_like(target[n + 1])

        def step(i):
            even = target[2 * i + 1]
            middle = dx[i + 1]
            after = sx[i + 1] - 0.25 * (middle + dx[i + 2])
            target[2 * i + 3] = after
            odd = middle + 0.5 * (even + after)
            target[2 * i + 2] = odd
            if emit is not None:
                emit(2 * i, even)
                emit(2 * i + 1, odd)

        each(h - 1, step)
        even, after, middle = target[n - 1], target[n + 1], dx[h]
        odd = middle + 0.5 * (even + after)
        target[n] = odd
        if emit is not None:
            emit(n - 2, even)
            emit(n - 1, odd)

    mats_s5 = per[LEVELS * width]

    send(0)
    for k in range(LEVELS):
        receive(k)
        fill(k)
        lift_x(k)
        lift_smooth(k)
        if k + 1 < LEVELS:
            send(k + 1)
        lift_detail(k)
        weigh_bands(k)
        unlift_detail(k)
    lv = levels[-1]
    each(lv.h + 1, lambda i: weigh(mats_s5, i, 3 * LEVELS))

    def emit(x, value):
        tile = value[8 : 8 + rows_in].T
        xin[0, pl.ds(x, cells, stride=planes_in), :] = tile[:cells]
        xin[1, pl.ds(x, cells, stride=planes_in), :] = tile[cells:]

    coarse = mats_s5
    for k in reversed(range(LEVELS)):
        unlift_smooth(k, coarse)
        for copy in copies(k):
            copy.wait_send()
        coarse = lv_refs[k][0]
        unlift_x(k, coarse, emit if k == 0 else None)

    stores = [
        pltpu.make_async_copy(
            xin.at[side], out_ref.at[:, side * rows_in : (side + 1) * rows_in], in_sem.at[side]
        )
        for side in range(2)
    ]
    for store in stores:
        store.start()
    for store in stores:
        store.wait()


def per_device(counts, control, band_roots):
    vectors, layers, planes, cols = control.shape
    rows = cols // 2
    levels = levels_of(planes, rows)
    cells = vectors * layers
    x = control.reshape(cells * planes, cols)
    scratch = [
        pltpu.VMEM((2, cells * planes, rows), F32),
        pltpu.VMEM((16, 256, 256), BF16),
        pltpu.SemaphoreType.DMA((2,)),
        pltpu.SemaphoreType.DMA((LEVELS, 12)),
        pltpu.SemaphoreType.DMA((LEVELS, 12)),
    ]
    for lv in levels:
        scratch += [
            pltpu.VMEM((lv.n + 4, lv.r, 128), F32),
            pltpu.VMEM((2, lv.y, 128), F32),
            pltpu.VMEM((2, lv.sent, 128), F32),
            pltpu.VMEM((1, lv.sent, 128), F32),
            pltpu.VMEM((2, lv.got, 128), F32),
            pltpu.VMEM((1, lv.got, 128), F32),
            pltpu.VMEM((lv.h + 1, lv.r, 128), F32),
            pltpu.VMEM((lv.h + 2, lv.r, 128), F32),
            pltpu.VMEM((lv.h + 1, lv.rb, 128), F32),
            pltpu.VMEM((lv.h + 2, lv.rb, 128), F32),
            pltpu.VMEM((lv.h + 2, lv.rb, 128), F32),
        ]
    scratch.append(pltpu.VMEM((levels[-1].h + 1, levels[-1].rb, 128), F32))
    out = pl.pallas_call(
        partial(kernel, levels, counts),
        out_shape=jax.ShapeDtypeStruct((cells * planes, cols), F32),
        in_specs=[
            pl.BlockSpec(memory_space=pl.ANY),
            pl.BlockSpec(memory_space=pltpu.VMEM),
        ],
        out_specs=pl.BlockSpec(memory_space=pl.ANY),
        scratch_shapes=scratch,
        compiler_params=pltpu.CompilerParams(
            collective_id=0, has_side_effects=True, vmem_limit_bytes=48 << 20
        ),
        name="wavelet",
    )(x, band_roots)
    return out.reshape(control.shape)


def solution(mesh):
    counts = (mesh.shape["gx"], mesh.shape["gy"])
    in_specs = (P(None, None, "gx", "gy"), P())
    out_specs = P(None, None, "gx", "gy")
    return jax.shard_map(
        partial(per_device, counts),
        mesh=mesh,
        in_specs=in_specs,
        out_specs=out_specs,
        check_vma=False,
    )
```

profile of v0, /device:TPU:1, one launch (start us, length us, event | category | flops | bytes accessed | tf_op | source)
XLA Modules:
  0.0 56.1 jit_solution(652443762601557990)
XLA Ops:
  0.0 0.0 copy-start
  0.0 1.6 %copy-done = f32[2,32,32,256]{3,2,1,0:T(8,128)S(1)} copy-done((f32[2,32,32,256]{3,2,1,0:T(8,128)S(1)}, f32[2,32,32,256]{3,2,1,0:T(8,128)}, u32[]{:S(2)}) %copy-start) | copy-done | bytes 2097176
  1.6 0.0 copy-start.1
  1.6 0.9 %copy-done.1 = f32[16,32,32]{2,1,0:T(8,128)S(1)} copy-done((f32[16,32,32]{2,1,0:T(8,128)S(1)}, f32[16,32,32]{2,1,0:T(8,128)}, u32[]{:S(2)}) %copy-start.1) | copy-done | bytes 65560
  2.5 52.3 %wavelet.1 = f32[2048,256]{1,0:T(8,128)S(1)} custom-call(f32[2048,256]{1,0:T(8,128)S(1)} %bitcast.3, f32[16,32,32]{2,1,0:T(8,128)S(1)} %copy-done.1), custom_call_target="tpu_custom_call" | custom-call | tf_op jit(solution)/shard_map/wavelet/pallas_call | solution.py:436
  54.8 1.3 %copy.4 = f32[2,32,32,256]{3,2,1,0:T(8,128)} copy(f32[2,32,32,256]{3,2,1,0:T(8,128)S(1)} %bitcast.2) | data formatting | bytes 4194304
Async XLA Ops:
  0.0 1.6 %copy-start = (f32[2,32,32,256]{3,2,1,0:T(8,128)S(1)}, f32[2,32,32,256]{3,2,1,0:T(8,128)}, u32[]{:S(2)}) copy-start(f32[2,32,32,256]{3,2,1,0:T(8,128)} %param.2) | copy-start | bytes 6291460
  1.6 0.9 %copy-start.1 = (f32[16,32,32]{2,1,0:T(8,128)S(1)}, f32[16,32,32]{2,1,0:T(8,128)}, u32[]{:S(2)}) copy-start(f32[16,32,32]{2,1,0:T(8,128)} %w_ref.1) | copy-start | bytes 196612
where the time goes:
time: 56.6 us; the launch traced here: 56.1 us
  Pallas kernels  52.3 us (92%)
  local copies, waits for them, and re-layouts  3.86 us (7%)
    pallas_call x1, Pallas kernels, per_device(): pl.pallas_call(partial(kernel, levels, counts), out_shape=jax.ShapeDtypeS...  52.3 us
    unnamed x5, local copies, waits for them, and re-layouts  3.86 us

commit v1 on v0

--- a/solution.py
+++ b/solution.py
@@ -45,10 +45,10 @@
             body(i)
 
 
-def kernel(levels, counts, x_hbm, w_ref, out_ref, *scratch):
+def kernel(levels, counts, x_hbm, w_hbm, out_ref, *scratch):
     count_x, count_y = counts
-    (xin, mats, in_sem, send_sem, recv_sem) = scratch[:5]
-    per = scratch[5:]
+    (xin, w_ref, mats, in_sem, send_sem, recv_sem) = scratch[:6]
+    per = scratch[6:]
     width = 11
     lv_refs = [per[k * width : (k + 1) * width] for k in range(LEVELS)]
     gx = lax.axis_index("gx")
@@ -73,6 +73,7 @@
             barrier, inc=1, device_id=at(dx, dy), device_id_type=pl.DeviceIdType.MESH
         )
 
+    w_load = pltpu.make_async_copy(w_hbm, w_ref, in_sem.at[2])
     loads = [
         pltpu.make_async_copy(
             x_hbm.at[:, side * rows_in : (side + 1) * rows_in], xin.at[side], in_sem.at[side]
@@ -81,6 +82,7 @@
     ]
     for load in loads:
         load.start()
+    w_load.start()
 
     lane = lax.broadcasted_iota(jnp.int32, (1, 128), 1)
     upper = lane >= 64
@@ -101,8 +103,6 @@
         mats[band, 128:256, 0:128] = high
         mats[band, 0:128, 128:256] = low
         mats[band, 128:256, 128:256] = jnp.zeros((128, 128), BF16)
-
-    each(16, build)
 
     for load in loads:
         load.wait()
@@ -138,8 +138,9 @@
         for source, target, dx in groups:
             moves.append((en.at[:, source], rn.at[:, target], (dx, -1)))
             moves.append((es.at[:, source], rs.at[:, target], (dx, 1)))
-        return [
-            pltpu.make_async_remote_copy(
+        ways = {}
+        for m, (source, target, way) in enumerate(moves):
+            copy = pltpu.make_async_remote_copy(
                 src_ref=source,
                 dst_ref=target,
                 send_sem=send_sem.at[k, m],
@@ -147,8 +148,39 @@
                 device_id=at(*way),
                 device_id_type=pl.DeviceIdType.MESH,
             )
-            for m, (source, target, way) in enumerate(moves)
-        ]
+            ways.setdefault(way, []).append(copy)
+        return ways
+
+    def exists(dx, dy):
+        x, y = gx + dx, gy + dy
+        inside_x = jnp.logical_and(x >= 0, x < count_x)
+        return jnp.logical_and(inside_x, jnp.logical_and(y >= 0, y < count_y))
+
+    def start(ways, wanted):
+        for way, group in ways.items():
+            if wanted(*way):
+
+                @pl.when(exists(*way))
+                def _():
+                    for copy in group:
+                        copy.start()
+
+    def arrive(ways, wanted):
+        for (dx, dy), group in ways.items():
+            if wanted(dx, dy):
+
+                @pl.when(exists(-dx, -dy))
+                def _():
+                    for copy in group:
+                        copy.wait_recv()
+
+    def sent(ways):
+        for way, group in ways.items():
+
+            @pl.when(exists(*way))
+            def _():
+                for copy in group:
+                    copy.wait_send()
 
     def send(k):
         lv = levels[k]
@@ -159,61 +191,53 @@
         if not lv.short:
             sp[0] = a[2, rows] - 0.5 * (a[1, rows] + a[3, rows])
         sp[1] = a[n, rows] - 0.5 * a[n - 1, rows]
-        x_moves = 4 if lv.short else 3
-        for copy in todo[:x_moves]:
-            copy.start()
-
-        def edge(x):
-            one = pl.ds(x, 1)
-            r0, r1, r2 = a[x + 1, 8:9], a[x + 1, 9:10], a[x + 1, 10:11]
-            before, end = a[x + 1, y + 6 : y + 7], a[x + 1, y + 7 : y + 8]
-            en[0, one] = r0
-            en[1, one] = r1 - 0.5 * (r0 + r2)
-            es[0, one] = end - 0.5 * before
-
-        each(n, edge, 8)
-        for ref, kinds in ((en, 2), (es, 1)):
-            for kind in range(kinds):
-                row = lambda i: ref[kind, i : i + 1]
-                ref[kind, lv.npad : lv.npad + 1] = row(0)
-                second = row(1) if lv.short else row(1) - 0.5 * (row(0) + row(2))
-                ref[kind, lv.npad + 1 : lv.npad + 2] = second
-                ref[kind, lv.npad + 8 : lv.npad + 9] = row(n - 1) - 0.5 * row(n - 2)
-        for copy in todo[x_moves:]:
-            copy.start()
-
-    def receive(k):
-        for copy in copies(k):
-            copy.wait_recv()
+        start(todo, lambda dx, dy: dy == 0)
+        flat = a.reshape((lv.n + 4) * lv.r, 128)
+        line = lambda row: flat[pl.ds(lv.r + row, n, stride=lv.r), :]
+        r0 = line(8)
+        f_edge, d_edge = r0, line(9) - 0.5 * (r0 + line(10))
+        q_edge = line(y + 7) - 0.5 * line(y + 6)
+        for ref, kind, edge in ((en, 0, f_edge), (en, 1, d_edge), (es, 0, q_edge)):
+            ref[kind, 0:n] = edge
+            row = lambda i: ref[kind, i : i + 1]
+            ref[kind, lv.npad : lv.npad + 1] = row(0)
+            second = row(1) if lv.short else row(1) - 0.5 * (row(0) + row(2))
+            ref[kind, lv.npad + 1 : lv.npad + 2] = second
+            ref[kind, lv.npad + 8 : lv.npad + 9] = row(n - 1) - 0.5 * row(n - 2)
+        start(todo, lambda dx, dy: dy != 0)
+
+    def turn(value):
+        return pltpu.roll(value, 64, 1)
 
     def fill(k):
         lv = levels[k]
         a, sp, en, es, rn, rs = lv_refs[k][:6]
         n, y = lv.n, lv.y
-
-        def place(plane, f_here, d_here, q_here, slot):
-            f_there, d_there, q_there = rn[0, slot], rn[1, slot], rs[0, slot]
-            turn = lambda value: pltpu.roll(value, 64, 1)
-            a[plane, y + 8 : y + 9] = jnp.where(
-                keep_next, turn(jnp.where(upper, f_here, f_there)), 0.0
-            )
-            a[plane, y + 9 : y + 10] = jnp.where(
-                keep_next, turn(jnp.where(upper, d_here, d_there)), 0.0
-            )
-            a[plane, 7:8] = turn(jnp.where(upper, q_there, q_here))
-
-        def local(x):
-            one = pl.ds(x, 1)
-            place(x + 1, en[0, one], en[1, one], es[0, one], one)
-
-        each(n, local, 8)
+        todo = copies(k)
+        flat = a.reshape((lv.n + 4) * lv.r, 128)
+
+        def place(plane, count, f_here, d_here, q_here, slot):
+            slot = pl.ds(slot, count)
+
+            def put(row, value):
+                flat[pl.ds(plane * lv.r + row, count, stride=lv.r), :] = value
+
+            f_all = turn(jnp.where(upper, f_here, rn[0, slot]))
+            d_all = turn(jnp.where(upper, d_here, rn[1, slot]))
+            put(y + 8, jnp.where(keep_next, f_all, 0.0))
+            put(y + 9, jnp.where(keep_next, d_all, 0.0))
+            put(7, turn(jnp.where(upper, rs[0, slot], q_here)))
+
+        arrive(todo, lambda dx, dy: dx == 0)
+        place(1, n, en[0, 0:n], en[1, 0:n], es[0, 0:n], 0)
+        arrive(todo, lambda dx, dy: dx != 0)
         halo = [(n + 1, lv.npad), (n + 2, lv.npad + 1), (0, lv.npad + 8)]
         if lv.short:
             halo.append((n + 3, lv.npad + 16))
         for plane, slot in halo:
             r0, r1, r2 = a[plane, 8:9], a[plane, 9:10], a[plane, 10:11]
             before, end = a[plane, y + 6 : y + 7], a[plane, y + 7 : y + 8]
-            place(plane, r0, r1 - 0.5 * (r0 + r2), end - 0.5 * before, pl.ds(slot, 1))
+            place(plane, 1, r0, r1 - 0.5 * (r0 + r2), end - 0.5 * before, slot)
         if lv.short:
 
             @pl.when(gx == count_x - 2)
@@ -291,20 +315,26 @@
 
         each(lv.h + 2, step)
 
-    def weigh(ref, i, band):
-        value = ref[i]
-        high = value.astype(BF16)
-        low = (value - high.astype(F32)).astype(BF16)
-        both = jnp.concatenate([high, low], axis=1)
-        product = jnp.dot(both, mats[band], preferred_element_type=F32)
-        ref[i] = product[:, :128] + product[:, 128:]
+    def weigh(ref, band, most=512):
+        planes, rows, _ = ref.shape
+        chunk = planes
+        while chunk * rows > most and chunk % 3 == 0:
+            chunk //= 3
+
+        def step(i):
+            value = ref[pl.ds(i * chunk, chunk)].reshape(chunk * rows, 128)
+            high = value.astype(BF16)
+            low = (value - high.astype(F32)).astype(BF16)
+            both = jnp.concatenate([high, low], axis=1)
+            product = jnp.dot(both, mats[band], preferred_element_type=F32)
+            total = product[:, :128] + product[:, 128:]
+            ref[pl.ds(i * chunk, chunk)] = total.reshape(chunk, rows, 128)
+
+        each(planes // chunk, step, 1)
 
     def weigh_bands(k):
-        lv = levels[k]
-        b0, b1, b2 = lv_refs[k][8:11]
-        each(lv.h + 1, lambda i: weigh(b0, i, 3 * k))
-        each(lv.h + 2, lambda i: weigh(b1, i, 3 * k + 1))
-        each(lv.h + 2, lambda i: weigh(b2, i, 3 * k + 2))
+        for offset in range(3):
+            weigh(lv_refs[k][8 + offset], 3 * k + offset)
 
     def unlift_y(lv, smooth, detail, plane):
         hy, y = lv.hy, lv.y
@@ -367,8 +397,9 @@
     mats_s5 = per[LEVELS * width]
 
     send(0)
+    w_load.wait()
+    each(16, build)
     for k in range(LEVELS):
-        receive(k)
         fill(k)
         lift_x(k)
         lift_smooth(k)
@@ -377,32 +408,20 @@
         lift_detail(k)
         weigh_bands(k)
         unlift_detail(k)
-    lv = levels[-1]
-    each(lv.h + 1, lambda i: weigh(mats_s5, i, 3 * LEVELS))
+    weigh(mats_s5, 3 * LEVELS)
 
     def emit(x, value):
         tile = value[8 : 8 + rows_in].T
-        xin[0, pl.ds(x, cells, stride=planes_in), :] = tile[:cells]
-        xin[1, pl.ds(x, cells, stride=planes_in), :] = tile[cells:]
+        base = (x // 8) * 16 + lax.rem(x, 8)
+        out_ref[pl.ds(base, cells, stride=2 * planes_in), :] = tile[:cells]
+        out_ref[pl.ds(base + 8, cells, stride=2 * planes_in), :] = tile[cells:]
 
     coarse = mats_s5
     for k in reversed(range(LEVELS)):
         unlift_smooth(k, coarse)
-        for copy in copies(k):
-            copy.wait_send()
+        sent(copies(k))
         coarse = lv_refs[k][0]
         unlift_x(k, coarse, emit if k == 0 else None)
-
-    stores = [
-        pltpu.make_async_copy(
-            xin.at[side], out_ref.at[:, side * rows_in : (side + 1) * rows_in], in_sem.at[side]
-        )
-        for side in range(2)
-    ]
-    for store in stores:
-        store.start()
-    for store in stores:
-        store.wait()
 
 
 def per_device(counts, control, band_roots):
@@ -413,8 +432,9 @@
     x = control.reshape(cells * planes, cols)
     scratch = [
         pltpu.VMEM((2, cells * planes, rows), F32),
+        pltpu.VMEM(band_roots.shape, F32),
         pltpu.VMEM((16, 256, 256), BF16),
-        pltpu.SemaphoreType.DMA((2,)),
+        pltpu.SemaphoreType.DMA((3,)),
         pltpu.SemaphoreType.DMA((LEVELS, 12)),
         pltpu.SemaphoreType.DMA((LEVELS, 12)),
     ]
@@ -428,25 +448,26 @@
             pltpu.VMEM((1, lv.got, 128), F32),
             pltpu.VMEM((lv.h + 1, lv.r, 128), F32),
             pltpu.VMEM((lv.h + 2, lv.r, 128), F32),
-            pltpu.VMEM((lv.h + 1, lv.rb, 128), F32),
+            pltpu.VMEM((lv.h + 2, lv.rb, 128), F32),
             pltpu.VMEM((lv.h + 2, lv.rb, 128), F32),
             pltpu.VMEM((lv.h + 2, lv.rb, 128), F32),
         ]
     scratch.append(pltpu.VMEM((levels[-1].h + 1, levels[-1].rb, 128), F32))
     out = pl.pallas_call(
         partial(kernel, levels, counts),
-        out_shape=jax.ShapeDtypeStruct((cells * planes, cols), F32),
+        out_shape=jax.ShapeDtypeStruct((cells * planes * 2, rows), F32),
         in_specs=[
-            pl.BlockSpec(memory_space=pl.ANY),
-            pl.BlockSpec(memory_space=pltpu.VMEM),
+            pl.BlockSpec(memory_space=pltpu.HBM),
+            pl.BlockSpec(memory_space=pltpu.HBM),
         ],
-        out_specs=pl.BlockSpec(memory_space=pl.ANY),
+        out_specs=pl.BlockSpec(memory_space=pltpu.VMEM),
         scratch_shapes=scratch,
         compiler_params=pltpu.CompilerParams(
-            collective_id=0, has_side_effects=True, vmem_limit_bytes=48 << 20
+            collective_id=0, has_side_effects=True, vmem_limit_bytes=54000000
         ),
         name="wavelet",
     )(x, band_roots)
+    out = out.reshape(cells * planes // 8, 2, 8, rows).transpose(0, 2, 1, 3)
     return out.reshape(control.shape)
 
 

time: 56.6 us -> 40 us (0.71)
  the two profiles are of different devices: /device:TPU:1 before, /device:TPU:7 now
where the time goes in v1:
time: 40 us; the launch traced here: 39.9 us
  Pallas kernels  37.6 us (94%)
  local copies, waits for them, and re-layouts  2.27 us (6%)
    pallas_call x1, Pallas kernels, per_device(): pl.pallas_call(partial(kernel, levels, counts), out_shape=jax.ShapeDtypeS...  37.6 us
    unnamed x3, local copies, waits for them, and re-layouts  2.27 us

profile of v1, /device:TPU:7, one launch (start us, length us, event | category | flops | bytes accessed | tf_op | source)
XLA Modules:
  0.0 39.9 jit_solution(8022201950720519660)
XLA Ops:
  0.0 0.0 copy-start
  0.0 0.9 %copy-done = f32[16,32,32]{2,1,0:T(8,128)S(1)} copy-done((f32[16,32,32]{2,1,0:T(8,128)S(1)}, f32[16,32,32]{2,1,0:T(8,128)}, u32[]{:S(2)}) %copy-start) | copy-done | bytes 65560
  1.0 37.6 %wavelet.1 = f32[4096,128]{1,0:T(8,128)S(1)} custom-call(f32[2048,256]{1,0:T(8,128)} %bitcast.7, f32[16,32,32]{2,1,0:T(8,128)S(1)} %copy-done), custom_call_target="tpu_custom_call" | custom-call | tf_op jit(solution)/shard_map/wavelet/pallas_call | solution.py:456
  38.6 1.3 %copy.4 = f32[2,32,32,256]{3,2,1,0:T(8,128)} copy(f32[2,32,32,256]{3,2,1,0:T(8,128)S(1)} %bitcast.6) | data formatting | bytes 4194304
Async XLA Ops:
  0.0 0.9 %copy-start = (f32[16,32,32]{2,1,0:T(8,128)S(1)}, f32[16,32,32]{2,1,0:T(8,128)}, u32[]{:S(2)}) copy-start(f32[16,32,32]{2,1,0:T(8,128)} %w_hbm.1) | copy-start | bytes 196612

commit v2 on v1

v2 whole, which is shorter than its diff:
```python
from functools import partial

import jax
import jax.numpy as jnp
from jax import lax
from jax.experimental import pallas as pl
from jax.experimental.pallas import tpu as pltpu
from jax.sharding import PartitionSpec as P

LEVELS = 5
F32 = jnp.float32
BF16 = jnp.bfloat16


def round_up(value, step):
    return (value + step - 1) // step * step


class Level:
    def __init__(self, planes, rows, first, last):
        self.n = planes
        self.y = rows
        self.h = planes // 2
        self.hy = rows // 2
        self.first = first
        self.last = last
        self.r = round_up(rows + 10, 8)
        self.rb = round_up(self.hy + 10, 16)
        self.rs = round_up(self.hy + 3, 8)
        self.hp = round_up(self.h + 3, 8)
        self.bands = 4 if last else 3
        self.kinds = ["sd", "ds", "dd", "ss"][: self.bands]
        self.reach = 2 if self.h == 1 else 1

    def x_strip(self, kind, hop):
        low = -1 if kind == "d" else 0
        high = self.h + (1 if kind == "s" else 0)
        begin = max(low, -1 - hop * self.h)
        end = min(self.h, high - hop * self.h)
        return begin + hop * self.h, begin, end - begin + 1

    def y_rows(self, kind, hop):
        if hop < 0:
            return -1, self.hy - 1
        return (self.hy - 1, -1) if kind == "d" else (self.hy, 0)


def levels_of(planes, rows):
    return [
        Level(planes >> k, rows >> k, k == 0, k == LEVELS - 1) for k in range(LEVELS)
    ]


def each(count, body, unroll_to=4):
    if count <= unroll_to:
        for i in range(count):
            body(i)
    else:

        @pl.loop(0, count)
        def _(i):
            body(i)


NAMES = (
    "a",
    "sx",
    "dx",
    "b0",
    "b1",
    "b2",
    "b3",
    "yl",
    "yr",
    "ryl",
    "ryr",
    "cs",
    "cr",
    "xsl",
    "xsr",
    "xrl",
    "xrr",
    "xfs",
    "xfr",
)


def kernel(levels, counts, x_hbm, w_hbm, out_ref, *scratch):
    count_x, count_y = counts
    (xin, w_ref, mats, temp, in_sem, send_sem, recv_sem) = scratch[:7]
    per = scratch[7:]
    refs = [
        dict(zip(NAMES, per[k * len(NAMES) : (k + 1) * len(NAMES)])) for k in range(LEVELS)
    ]
    gx = lax.axis_index("gx")
    gy = lax.axis_index("gy")
    first_x, last_x = gx == 0, gx == count_x - 1
    planes_in = levels[0].n
    rows_in = levels[0].y
    cells = xin.shape[1] // planes_in

    def at(dx, dy):
        return {
            "gx": lax.rem(gx + dx + count_x, count_x),
            "gy": lax.rem(gy + dy + count_y, count_y),
        }

    friends = [
        (dx, dy) for dx in (-2, -1, 0, 1, 2) for dy in (-1, 0, 1) if (dx, dy) != (0, 0)
    ]
    barrier = pltpu.get_barrier_semaphore()
    for dx, dy in friends:
        pl.semaphore_signal(
            barrier, inc=1, device_id=at(dx, dy), device_id_type=pl.DeviceIdType.MESH
        )
    w_load = pltpu.make_async_copy(w_hbm, w_ref, in_sem.at[2])
    loads = [
        pltpu.make_async_copy(
            x_hbm.at[:, side * rows_in : (side + 1) * rows_in], xin.at[side], in_sem.at[side]
        )
        for side in range(2)
    ]
    for load in loads:
        load.start()
    w_load.start()

    lane = lax.broadcasted_iota(jnp.int32, (1, 128), 1)
    upper = lane >= 64
    keep_next = jnp.logical_or(lane < 64, gy < count_y - 1)
    keep_prev = jnp.logical_or(lane >= 64, gy > 0)
    not_first = jnp.where(first_x, 0.0, 1.0).astype(F32)

    block_row = lax.broadcasted_iota(jnp.int32, (128, 128), 0) // 32
    block_lane = lax.broadcasted_iota(jnp.int32, (128, 128), 1) // 32
    diagonal = block_row == block_lane

    def build(band):
        small = jnp.concatenate([w_ref[band]] * 4, axis=1)
        tiled = jnp.concatenate([small] * 4, axis=0)
        square = jnp.where(diagonal, tiled, 0.0).T
        high = square.astype(BF16)
        low = (square - high.astype(F32)).astype(BF16)
        mats[band, 0:128, 0:128] = high
        mats[band, 128:256, 0:128] = high
        mats[band, 0:128, 128:256] = low
        mats[band, 128:256, 128:256] = jnp.zeros((128, 128), BF16)

    def rows_of(ref, plane, count, row):
        planes, height, _ = ref.shape
        flat = ref.reshape(planes * height, 128)
        return flat, pl.ds(plane * height + row, count, stride=height)

    def gather(ref, plane, count, row):
        flat, where = rows_of(ref, plane, count, row)
        return flat[where, :]

    def scatter(ref, plane, count, row, value):
        flat, where = rows_of(ref, plane, count, row)
        flat[where, :] = value

    top = refs[0]["a"]
    for plane in (0, planes_in + 1, planes_in + 2):
        top[plane] = jnp.zeros(top.shape[1:], F32)
    for row in (7, rows_in + 8, rows_in + 9):
        scatter(top, 1, planes_in, row, jnp.zeros((planes_in, 128), F32))

    edge_right, edge_left = refs[0]["xrr"], refs[0]["xrl"]
    for edge in (edge_right, edge_left):
        for plane in range(edge.shape[0]):
            edge[plane, 0:8] = jnp.zeros((8, 128), F32)
            edge[plane, rows_in + 8 : rows_in + 16] = jnp.zeros((8, 128), F32)

    for load in loads:
        load.wait()

    def take(x):
        low = xin[0, pl.ds(x, cells, stride=planes_in), :]
        high = xin[1, pl.ds(x, cells, stride=planes_in), :]
        tile = jnp.concatenate([low, high], axis=0)
        top[x + 1, 8 : 8 + rows_in, :] = tile.T

    def copies(k):
        lv, r = levels[k], refs[k]
        landing = pl.ds(8, rows_in) if lv.first else pl.ds(0, lv.rs)
        moves = [
            (r["xsl"], r["xrr"].at[:, landing], (-1, 0)),
            (r["xsr"], r["xrl"].at[:, landing], (1, 0)),
        ]
        if lv.reach == 2:
            moves.append((r["xfs"].at[0], r["xfr"].at[0], (-2, 0)))
            moves.append((r["xfs"].at[1], r["xfr"].at[1], (2, 0)))
        moves.append((r["yl"], r["ryl"], (0, -1)))
        moves.append((r["yr"], r["ryr"], (0, 1)))
        for i, (hop, way) in enumerate(corners(lv)):
            moves.append((r["cs"].at[i], r["cr"].at[i], (hop, way)))
        ways = {}
        for m, (source, target, way) in enumerate(moves):
            copy = pltpu.make_async_remote_copy(
                src_ref=source,
                dst_ref=target,
                send_sem=send_sem.at[k, m],
                recv_sem=recv_sem.at[k, m],
                device_id=at(*way),
                device_id_type=pl.DeviceIdType.MESH,
            )
            ways.setdefault(way, []).append(copy)
        return ways

    def exists(dx, dy):
        x, y = gx + dx, gy + dy
        inside_x = jnp.logical_and(x >= 0, x < count_x)
        return jnp.logical_and(inside_x, jnp.logical_and(y >= 0, y < count_y))

    def start(ways, wanted):
        for way, group in ways.items():
            if wanted(*way):

                @pl.when(exists(*way))
                def _():
                    for copy in group:
                        copy.start()

    def arrive(ways):
        for (dx, dy), group in ways.items():

            @pl.when(exists(-dx, -dy))
            def _():
                for copy in group:
                    copy.wait_recv()

    def sent(ways):
        for way, group in ways.items():

            @pl.when(exists(*way))
            def _():
                for copy in group:
                    copy.wait_send()

    def send_first():
        n, rows = planes_in, pl.ds(8, rows_in)
        low, high = refs[0]["xsl"], refs[0]["xsr"]
        low[0] = top[1, rows]
        low[1] = top[2, rows] - 0.5 * (top[1, rows] + top[3, rows])
        high[0] = top[n, rows] - 0.5 * top[n - 1, rows]
        start(copies(0), lambda dx, dy: dy == 0)

    def send(k):
        lv, r = levels[k], refs[k]
        todo = copies(k)
        if not lv.first:
            whole, part = slice(7, lv.hy + 10), slice(0, lv.hy + 3)
            for name, low, single in (("xsl", 0, 1), ("xsr", lv.h, lv.h + 1)):
                for i in range(2):
                    r[name][i, part] = r["b1"][low + i, whole]
                    r[name][2 + i, part] = r["b2"][low + i, whole]
                r[name][4, part] = r["b0"][single, whole]
                if lv.last:
                    r[name][5, part] = r["b3"][single, whole]
            if lv.reach == 2:
                for place, plane in ((0, 0), (1, lv.h + 1)):
                    for t in (1, 2):
                        r["xfs"][place, t - 1, part] = r[f"b{t}"][plane, whole]
            start(todo, lambda dx, dy: dy == 0)
        planes = lv.h + 3
        for t, kind in enumerate(lv.kinds):
            for name, hop in (("yl", -1), ("yr", 1)):
                source, _ = lv.y_rows(kind[1], hop)
                for i in range(2):
                    count = planes if kind[0] == "s" else planes - 1
                    value = gather(r[f"b{t}"], 0, count, 8 + source + i)
                    r[name][2 * t + i, 0:count] = value
        for c, (hop, way) in enumerate(corners(lv)):
            strips = r["yl"] if way < 0 else r["yr"]
            for t, kind in enumerate(lv.kinds):
                source, _, count = lv.x_strip(kind[0], hop)
                planes = slice(source + 1, source + 1 + count)
                one, two = strips[2 * t, planes], strips[2 * t + 1, planes]
                if way < 0:
                    both = jnp.where(upper, pltpu.roll(two, 64, 1), one)
                else:
                    both = jnp.where(upper, two, pltpu.roll(one, 64, 1))
                r["cs"][c, 2 * t : 2 * t + count] = both
        start(todo, lambda dx, dy: dy != 0)

    def collect(k):
        lv, r = levels[k], refs[k]
        h = lv.h
        todo = copies(k)
        arrive(todo)
        whole, part = slice(7, lv.hy + 10), slice(0, lv.hy + 3)

        def add(t, position, value):
            r[f"b{t}"][position + 1, whole] = r[f"b{t}"][position + 1, whole] + value

        if lv.first:
            smooth_of = lambda i: temp[2 * i, whole]
            detail_of = lambda i: temp[2 * i + 1, whole]

            @pl.when(gx > 0)
            def _():
                lift_y(lv, edge_left.at[0], temp.at[0], temp.at[1], False)
                add(1, -1, smooth_of(0))
                add(2, -1, detail_of(0))
                add(0, 0, 0.25 * detail_of(0))

            @pl.when(gx < count_x - 1)
            def _():
                for i in range(2):
                    out = 2 + 2 * i
                    lift_y(lv, edge_right.at[i], temp.at[out], temp.at[out + 1], False)
                add(1, h - 1, -0.5 * smooth_of(1))
                add(2, h - 1, -0.5 * detail_of(1))
                add(1, h, smooth_of(2))
                add(2, h, detail_of(2))
                add(0, h - 1, -0.125 * detail_of(1))
                add(0, h, 0.875 * detail_of(1) + 0.25 * detail_of(2))

        else:
            smooth = [(0, 4, 2)] if lv.bands == 3 else [(0, 4, 2), (3, 5, 0)]
            from_left = lambda i: r["xrl"][i, part]
            from_right = lambda i: r["xrr"][i, part]

            @pl.when(gx > 0)
            def _():
                for t in (1, 2):
                    add(t, -1, from_left(2 * t - 2))
                    add(t, 0, from_left(2 * t - 1))
                for t, slot, d in smooth:
                    add(t, 0, from_left(slot))
                    add(t, 1, 0.25 * from_left(d + 1))

            @pl.when(gx < count_x - 1)
            def _():
                for t in (1, 2):
                    add(t, h - 1, from_right(2 * t - 2))
                    add(t, h, from_right(2 * t - 1))
                for t, slot, d in smooth:
                    add(t, h - 1, 0.25 * from_right(d))
                    add(t, h, from_right(slot))

            if lv.reach == 2:
                far = lambda side, d: r["xfr"][side, d, part]

                @pl.when(gx > 1)
                def _():
                    for t in (1, 2):
                        add(t, -1, far(1, t - 1))
                    for t, _, d in smooth:
                        add(t, 0, 0.25 * far(1, d // 2))

                @pl.when(gx < count_x - 2)
                def _():
                    for t in (1, 2):
                        add(t, h, far(0, t - 1))
                    for t, _, d in smooth:
                        add(t, h, 0.25 * far(0, d // 2))

        for c, (hop, way) in enumerate(corners(lv)):
            strips = r["ryl"] if way < 0 else r["ryr"]

            @pl.when(exists(-hop, -way))
            def _():
                for t, kind in enumerate(lv.kinds):
                    _, target, count = lv.x_strip(kind[0], hop)
                    packed = r["cr"][c, 2 * t : 2 * t + count]
                    other = pltpu.roll(packed, 64, 1)
                    planes = slice(target + 1, target + 1 + count)
                    for i in range(2):
                        value = packed if (way < 0) == (i == 0) else other
                        strips[2 * t + i, planes] = strips[2 * t + i, planes] + value

        planes = h + 2
        for t, kind in enumerate(lv.kinds):
            band = r[f"b{t}"]
            todo_rows = []
            for i in range(2):
                source, target = lv.y_rows(kind[1], -1)
                here = gather(band, 0, planes, 8 + source + i)
                there = r["ryl"][2 * t + i, 0:planes]
                moved = pltpu.roll(jnp.where(upper, here, there), 64, 1)
                todo_rows.append((target + i, jnp.where(keep_next, moved, 0.0)))
                source, target = lv.y_rows(kind[1], 1)
                here = gather(band, 0, planes, 8 + source + i)
                there = r["ryr"][2 * t + i, 0:planes]
                moved = pltpu.roll(jnp.where(upper, there, here), 64, 1)
                todo_rows.append((target + i, jnp.where(keep_prev, moved, 0.0)))
            for row, value in todo_rows:
                mine = gather(band, 0, planes, 8 + row)
                scatter(band, 0, planes, 8 + row, mine + value)

    def lift_x(k):
        lv = levels[k]
        a, sx, dx = (refs[k][name] for name in ("a", "sx", "dx"))
        n, h = lv.n, lv.h
        low = not_first * (a[0] - 0.5 * a[1])
        dx[0] = low
        sx[0] = 0.25 * low

        def step(i):
            even = a[2 * i + 1]
            detail = a[2 * i + 2] - 0.5 * (even + a[2 * i + 3])
            dx[i + 1] = detail
            sx[i + 1] = even + 0.25 * (dx[i] + detail)

        each(h, step)
        high = a[n + 2] - 0.5 * a[n + 1]
        dx[h + 1] = high
        sx[h + 1] = a[n + 1] + 0.25 * (dx[h] + high)
        sx[h + 2] = 0.25 * high

    def lift_y(lv, plane, smooth, detail, mask):
        hy, y = lv.hy, lv.y
        even = plane[pl.ds(8, hy, stride=2), :]
        odd = plane[pl.ds(9, hy, stride=2), :]
        after = plane[pl.ds(10, hy, stride=2), :]
        fresh = odd - 0.5 * (even + after)
        detail[8 : 8 + hy] = fresh
        low = jnp.where(keep_prev, plane[7:8] - 0.5 * plane[8:9], 0.0)
        next_even = plane[y + 8 : y + 9]
        high = plane[y + 9 : y + 10] - 0.5 * next_even
        detail[7:8] = low
        detail[8 + hy : 9 + hy] = high
        smooth[8 : 8 + hy] = even + 0.25 * (detail[7 : 7 + hy] + fresh)
        smooth[7:8] = 0.25 * low
        end = next_even + 0.25 * (detail[7 + hy : 8 + hy] + high)
        end_next = 0.25 * high
        if mask:
            end = jnp.where(keep_next, end, 0.0)
            end_next = jnp.where(keep_next, end_next, 0.0)
        smooth[8 + hy : 9 + hy] = end
        smooth[9 + hy : 10 + hy] = end_next

    def lift_smooth(k):
        lv, r = levels[k], refs[k]
        coarse = r["b3"] if lv.last else refs[k + 1]["a"]
        each(
            lv.h + 3,
            lambda i: lift_y(lv, r["sx"].at[i], coarse.at[i], r["b0"].at[i], not lv.last),
        )
        if not lv.last:

            @pl.when(last_x)
            def _():
                coarse[lv.h + 1] = jnp.zeros_like(coarse[lv.h + 1])
                coarse[lv.h + 2] = jnp.zeros_like(coarse[lv.h + 2])

    def lift_detail(k):
        lv, r = levels[k], refs[k]
        each(
            lv.h + 2,
            lambda i: lift_y(lv, r["dx"].at[i], r["b1"].at[i], r["b2"].at[i], False),
        )

    def weigh(ref, band, begin, planes, most=512):
        rows = ref.shape[1]
        chunk = planes
        while chunk * rows > most and chunk % 3 == 0:
            chunk //= 3

        def step(i):
            part = pl.ds(begin + i * chunk, chunk)
            value = ref[part].reshape(chunk * rows, 128)
            high = value.astype(BF16)
            low = (value - high.astype(F32)).astype(BF16)
            both = jnp.concatenate([high, low], axis=1)
            product = jnp.dot(both, mats[band], preferred_element_type=F32)
            total = product[:, :128] + product[:, 128:]
            ref[part] = total.reshape(chunk, rows, 128)

        each(planes // chunk, step, 1)

    def weigh_bands(k):
        lv, r = levels[k], refs[k]
        for t in range(lv.bands):
            weigh(r[f"b{t}"], 3 * k + t, 0, lv.h + 2)

    def unlift_y(lv, smooth, detail, plane):
        hy, y = lv.hy, lv.y
        fresh = detail[8 : 8 + hy]
        even = smooth[8 : 8 + hy] - 0.25 * (detail[7 : 7 + hy] + fresh)
        plane[pl.ds(8, hy, stride=2), :] = even
        last = smooth[8 + hy : 9 + hy] - 0.25 * (
            detail[7 + hy : 8 + hy] + detail[8 + hy : 9 + hy]
        )
        plane[y + 8 : y + 9] = jnp.where(keep_next, last, 0.0)
        after = plane[pl.ds(10, hy, stride=2), :]
        plane[pl.ds(9, hy, stride=2), :] = fresh + 0.5 * (even + after)

    def unlift_detail(k):
        lv, r = levels[k], refs[k]
        each(lv.h + 2, lambda i: unlift_y(lv, r["b1"].at[i], r["b2"].at[i], r["dx"].at[i]))

    def unlift_smooth(k, coarse):
        lv, r = levels[k], refs[k]
        each(
            lv.h + 1,
            lambda i: unlift_y(lv, coarse.at[i + 1], r["b0"].at[i + 1], r["sx"].at[i + 1]),
        )

    def unlift_x(k, target, emit=None):
        lv = levels[k]
        sx, dx = refs[k]["sx"], refs[k]["dx"]
        n, h = lv.n, lv.h
        target[1] = sx[1] - 0.25 * (dx[0] + dx[1])

        @pl.when(jnp.logical_not(last_x))
        def _():
            target[n + 1] = sx[h + 1] - 0.25 * (dx[h] + dx[h + 1])

        @pl.when(last_x)
        def _():
            target[n + 1] = jnp.zeros_like(target[n + 1])

        def step(i):
            even = target[2 * i + 1]
            middle = dx[i + 1]
            after = sx[i + 2] - 0.25 * (middle + dx[i + 2])
            target[2 * i + 3] = after
            odd = middle + 0.5 * (even + after)
            target[2 * i + 2] = odd
            if emit is not None:
                emit(2 * i, even)
                emit(2 * i + 1, odd)

        each(h - 1, step)
        even, after, middle = target[n - 1], target[n + 1], dx[h]
        odd = middle + 0.5 * (even + after)
        target[n] = odd
        if emit is not None:
            emit(n - 2, even)
            emit(n - 1, odd)

    edge_planes = (0, 1, 2, planes_in - 2, planes_in - 1)
    for x in edge_planes:
        take(x)
    pl.semaphore_wait(barrier, len(friends))
    send_first()

    @pl.loop(0, (planes_in - len(edge_planes)) // 3)
    def _(i):
        for j in range(3):
            take(3 + 3 * i + j)

    for k in range(LEVELS):
        lift_x(k)
        lift_smooth(k)
        lift_detail(k)
        send(k)
    w_load.wait()
    each(16, build)
    for k in range(LEVELS):
        collect(k)
        weigh_bands(k)
        unlift_detail(k)

    def emit(x, value):
        tile = value[8 : 8 + rows_in].T
        base = (x // 8) * 16 + lax.rem(x, 8)
        out_ref[pl.ds(base, cells, stride=2 * planes_in), :] = tile[:cells]
        out_ref[pl.ds(base + 8, cells, stride=2 * planes_in), :] = tile[cells:]

    coarse = refs[LEVELS - 1]["b3"]
    for k in reversed(range(LEVELS)):
        unlift_smooth(k, coarse)
        coarse = refs[k]["a"]
        unlift_x(k, coarse, emit if k == 0 else None)
    for k in range(LEVELS):
        sent(copies(k))


def corners(lv):
    hops = [-1, 1] + ([-2, 2] if lv.reach == 2 else [])
    return [(hop, way) for way in (-1, 1) for hop in hops]


def per_device(counts, control, band_roots):
    vectors, layers, planes, cols = control.shape
    rows = cols // 2
    levels = levels_of(planes, rows)
    cells = vectors * layers
    x = control.reshape(cells * planes, cols)
    scratch = [
        pltpu.VMEM((2, cells * planes, rows), F32),
        pltpu.VMEM(band_roots.shape, F32),
        pltpu.VMEM((16, 256, 256), BF16),
        pltpu.VMEM((6, levels[0].rb, 128), F32),
        pltpu.SemaphoreType.DMA((3,)),
        pltpu.SemaphoreType.DMA((LEVELS, 24)),
        pltpu.SemaphoreType.DMA((LEVELS, 24)),
    ]
    for lv in levels:
        t, h = lv.bands, lv.h
        shapes = dict(
            a=(lv.n + 3, lv.r),
            sx=(h + 3, lv.r),
            dx=(h + 2, lv.r),
            b0=(h + 3, lv.rb),
            b1=(h + 2, lv.rb),
            b2=(h + 2, lv.rb),
            b3=(h + 3, lv.rb),
            yl=(2 * t, lv.hp),
            yr=(2 * t, lv.hp),
            ryl=(2 * t, lv.hp),
            ryr=(2 * t, lv.hp),
            cs=(len(corners(lv)), 8),
            cr=(len(corners(lv)), 8),
            xsl=(2, lv.y) if lv.first else (t + 2, lv.rs),
            xsr=(1, lv.y) if lv.first else (t + 2, lv.rs),
            xrl=(1, lv.y + 16) if lv.first else (t + 2, lv.rs),
            xrr=(2, lv.y + 16) if lv.first else (t + 2, lv.rs),
            xfs=(2, 2, lv.rs),
            xfr=(2, 2, lv.rs),
        )
        for name in NAMES:
            used = {"b3": lv.last, "xfs": lv.last, "xfr": lv.last}.get(name, True)
            scratch.append(pltpu.VMEM((shapes[name] if used else (8,)) + (128,), F32))
    out = pl.pallas_call(
        partial(kernel, levels, counts),
        out_shape=jax.ShapeDtypeStruct((cells * planes * 2, rows), F32),
        in_specs=[
            pl.BlockSpec(memory_space=pltpu.HBM),
            pl.BlockSpec(memory_space=pltpu.HBM),
        ],
        out_specs=pl.BlockSpec(memory_space=pltpu.VMEM),
        scratch_shapes=scratch,
        compiler_params=pltpu.CompilerParams(
            collective_id=0, has_side_effects=True, vmem_limit_bytes=54000000
        ),
        name="wavelet",
    )(x, band_roots)
    out = out.reshape(cells * planes // 8, 2, 8, rows).transpose(0, 2, 1, 3)
    return out.reshape(control.shape)


def solution(mesh):
    counts = (mesh.shape["gx"], mesh.shape["gy"])
    in_specs = (P(None, None, "gx", "gy"), P())
    out_specs = P(None, None, "gx", "gy")
    return jax.shard_map(
        partial(per_device, counts),
        mesh=mesh,
        in_specs=in_specs,
        out_specs=out_specs,
        check_vma=False,
    )
```

time: 40 us -> 29.6 us (0.74)
  the two profiles are of different devices: /device:TPU:7 before, /device:TPU:1 now
where the time goes in v2:
time: 29.6 us; the launch traced here: 29.4 us
  Pallas kernels  27.1 us (92%)
  local copies, waits for them, and re-layouts  2.27 us (8%)
    pallas_call x1, Pallas kernels, per_device(): pl.pallas_call(partial(kernel, levels, counts), out_shape=jax.ShapeDtypeS...  27.1 us
    unnamed x3, local copies, waits for them, and re-layouts  2.27 us

profile of v2, /device:TPU:1, one launch (start us, length us, event | category | flops | bytes accessed | tf_op | source)
XLA Modules:
  0.0 29.4 jit_solution(4089022675671221624)
XLA Ops:
  0.0 0.0 copy-start
  0.0 0.9 %copy-done = f32[16,32,32]{2,1,0:T(8,128)S(1)} copy-done((f32[16,32,32]{2,1,0:T(8,128)S(1)}, f32[16,32,32]{2,1,0:T(8,128)}, u32[]{:S(2)}) %copy-start) | copy-done | bytes 65560
  1.0 27.1 %wavelet.1 = f32[4096,128]{1,0:T(8,128)S(1)} custom-call(f32[2048,256]{1,0:T(8,128)} %bitcast.7, f32[16,32,32]{2,1,0:T(8,128)S(1)} %copy-done), custom_call_target="tpu_custom_call" | custom-call | tf_op jit(solution)/shard_map/wavelet/pallas_call | solution.py:617
  28.1 1.3 %copy.4 = f32[2,32,32,256]{3,2,1,0:T(8,128)} copy(f32[2,32,32,256]{3,2,1,0:T(8,128)S(1)} %bitcast.6) | data formatting | bytes 4194304
Async XLA Ops:
  0.0 0.9 %copy-start = (f32[16,32,32]{2,1,0:T(8,128)S(1)}, f32[16,32,32]{2,1,0:T(8,128)}, u32[]{:S(2)}) copy-start(f32[16,32,32]{2,1,0:T(8,128)} %w_hbm.1) | copy-start | bytes 196612

commit v3 on v2

--- a/solution.py
+++ b/solution.py
@@ -51,14 +51,19 @@
     ]
 
 
-def each(count, body, unroll_to=4):
+def each(count, body, unroll_to=4, group=1):
     if count <= unroll_to:
         for i in range(count):
             body(i)
     else:
-
-        @pl.loop(0, count)
+        rounds = count // group
+
+        @pl.loop(0, rounds)
         def _(i):
+            for j in range(group):
+                body(group * i + j)
+
+        for i in range(rounds * group, count):
             body(i)
 
 
@@ -169,6 +174,13 @@
         for plane in range(edge.shape[0]):
             edge[plane, 0:8] = jnp.zeros((8, 128), F32)
             edge[plane, rows_in + 8 : rows_in + 16] = jnp.zeros((8, 128), F32)
+
+    w_load.wait()
+
+    @pl.loop(0, 4)
+    def _(i):
+        for j in range(4):
+            build(4 * i + j)
 
     for load in loads:
         load.wait()
@@ -296,47 +308,38 @@
             smooth_of = lambda i: temp[2 * i, whole]
             detail_of = lambda i: temp[2 * i + 1, whole]
 
-            @pl.when(gx > 0)
-            def _():
-                lift_y(lv, edge_left.at[0], temp.at[0], temp.at[1], False)
-                add(1, -1, smooth_of(0))
-                add(2, -1, detail_of(0))
-                add(0, 0, 0.25 * detail_of(0))
-
-            @pl.when(gx < count_x - 1)
-            def _():
-                for i in range(2):
-                    out = 2 + 2 * i
-                    lift_y(lv, edge_right.at[i], temp.at[out], temp.at[out + 1], False)
-                add(1, h - 1, -0.5 * smooth_of(1))
-                add(2, h - 1, -0.5 * detail_of(1))
-                add(1, h, smooth_of(2))
-                add(2, h, detail_of(2))
-                add(0, h - 1, -0.125 * detail_of(1))
-                add(0, h, 0.875 * detail_of(1) + 0.25 * detail_of(2))
+            lift_y(lv, edge_left.at[0], temp.at[0], temp.at[1], False)
+            for i in range(2):
+                out = 2 + 2 * i
+                lift_y(lv, edge_right.at[i], temp.at[out], temp.at[out + 1], False)
+            for c, i in ((gx > 0, 0), (gx < count_x - 1, 1), (gx < count_x - 1, 2)):
+                temp[2 * i] = jnp.where(c, temp[2 * i], 0.0)
+                temp[2 * i + 1] = jnp.where(c, temp[2 * i + 1], 0.0)
+            add(1, -1, smooth_of(0))
+            add(2, -1, detail_of(0))
+            add(0, 0, 0.25 * detail_of(0))
+            add(1, h - 1, -0.5 * smooth_of(1))
+            add(2, h - 1, -0.5 * detail_of(1))
+            add(1, h, smooth_of(2))
+            add(2, h, detail_of(2))
+            add(0, h - 1, -0.125 * detail_of(1))
+            add(0, h, 0.875 * detail_of(1) + 0.25 * detail_of(2))
 
         else:
             smooth = [(0, 4, 2)] if lv.bands == 3 else [(0, 4, 2), (3, 5, 0)]
-            from_left = lambda i: r["xrl"][i, part]
-            from_right = lambda i: r["xrr"][i, part]
-
-            @pl.when(gx > 0)
-            def _():
-                for t in (1, 2):
-                    add(t, -1, from_left(2 * t - 2))
-                    add(t, 0, from_left(2 * t - 1))
-                for t, slot, d in smooth:
-                    add(t, 0, from_left(slot))
-                    add(t, 1, 0.25 * from_left(d + 1))
-
-            @pl.when(gx < count_x - 1)
-            def _():
-                for t in (1, 2):
-                    add(t, h - 1, from_right(2 * t - 2))
-                    add(t, h, from_right(2 * t - 1))
-                for t, slot, d in smooth:
-                    add(t, h - 1, 0.25 * from_right(d))
-                    add(t, h, from_right(slot))
+            from_left = lambda i: jnp.where(gx > 0, r["xrl"][i, part], 0.0)
+            from_right = lambda i: jnp.where(gx < count_x - 1, r["xrr"][i, part], 0.0)
+
+            for t in (1, 2):
+                add(t, -1, from_left(2 * t - 2))
+                add(t, 0, from_left(2 * t - 1))
+                add(t, h - 1, from_right(2 * t - 2))
+                add(t, h, from_right(2 * t - 1))
+            for t, slot, d in smooth:
+                add(t, 0, from_left(slot))
+                add(t, 1, 0.25 * from_left(d + 1))
+                add(t, h - 1, 0.25 * from_right(d))
+                add(t, h, from_right(slot))
 
             if lv.reach == 2:
                 far = lambda side, d: r["xfr"][side, d, part]
@@ -358,16 +361,15 @@
         for c, (hop, way) in enumerate(corners(lv)):
             strips = r["ryl"] if way < 0 else r["ryr"]
 
-            @pl.when(exists(-hop, -way))
-            def _():
-                for t, kind in enumerate(lv.kinds):
-                    _, target, count = lv.x_strip(kind[0], hop)
-                    packed = r["cr"][c, 2 * t : 2 * t + count]
-                    other = pltpu.roll(packed, 64, 1)
-                    planes = slice(target + 1, target + 1 + count)
-                    for i in range(2):
-                        value = packed if (way < 0) == (i == 0) else other
-                        strips[2 * t + i, planes] = strips[2 * t + i, planes] + value
+            there = exists(-hop, -way)
+            for t, kind in enumerate(lv.kinds):
+                _, target, count = lv.x_strip(kind[0], hop)
+                packed = jnp.where(there, r["cr"][c, 2 * t : 2 * t + count], 0.0)
+                other = pltpu.roll(packed, 64, 1)
+                planes = slice(target + 1, target + 1 + count)
+                for i in range(2):
+                    value = packed if (way < 0) == (i == 0) else other
+                    strips[2 * t + i, planes] = strips[2 * t + i, planes] + value
 
         planes = h + 2
         for t, kind in enumerate(lv.kinds):
@@ -402,7 +404,7 @@
             dx[i + 1] = detail
             sx[i + 1] = even + 0.25 * (dx[i] + detail)
 
-        each(h, step)
+        each(h, step, group=2)
         high = a[n + 2] - 0.5 * a[n + 1]
         dx[h + 1] = high
         sx[h + 1] = a[n + 1] + 0.25 * (dx[h] + high)
@@ -436,6 +438,7 @@
         each(
             lv.h + 3,
             lambda i: lift_y(lv, r["sx"].at[i], coarse.at[i], r["b0"].at[i], not lv.last),
+            group=3,
         )
         if not lv.last:
 
@@ -449,6 +452,7 @@
         each(
             lv.h + 2,
             lambda i: lift_y(lv, r["dx"].at[i], r["b1"].at[i], r["b2"].at[i], False),
+            group=3,
         )
 
     def weigh(ref, band, begin, planes, most=512):
@@ -488,13 +492,18 @@
 
     def unlift_detail(k):
         lv, r = levels[k], refs[k]
-        each(lv.h + 2, lambda i: unlift_y(lv, r["b1"].at[i], r["b2"].at[i], r["dx"].at[i]))
+        each(
+            lv.h + 2,
+            lambda i: unlift_y(lv, r["b1"].at[i], r["b2"].at[i], r["dx"].at[i]),
+            group=3,
+        )
 
     def unlift_smooth(k, coarse):
         lv, r = levels[k], refs[k]
         each(
             lv.h + 1,
             lambda i: unlift_y(lv, coarse.at[i + 1], r["b0"].at[i + 1], r["sx"].at[i + 1]),
+            group=3,
         )
 
     def unlift_x(k, target, emit=None):
@@ -522,7 +531,7 @@
                 emit(2 * i, even)
                 emit(2 * i + 1, odd)
 
-        each(h - 1, step)
+        each(h - 1, step, group=3)
         even, after, middle = target[n - 1], target[n + 1], dx[h]
         odd = middle + 0.5 * (even + after)
         target[n] = odd
@@ -533,21 +542,19 @@
     edge_planes = (0, 1, 2, planes_in - 2, planes_in - 1)
     for x in edge_planes:
         take(x)
-    pl.semaphore_wait(barrier, len(friends))
-    send_first()
-
     @pl.loop(0, (planes_in - len(edge_planes)) // 3)
     def _(i):
         for j in range(3):
             take(3 + 3 * i + j)
+
+    pl.semaphore_wait(barrier, len(friends))
+    send_first()
 
     for k in range(LEVELS):
         lift_x(k)
         lift_smooth(k)
         lift_detail(k)
         send(k)
-    w_load.wait()
-    each(16, build)
     for k in range(LEVELS):
         collect(k)
         weigh_bands(k)

time: 29.6 us -> 27.3 us (0.922)
  Pallas kernels: 27.1 us -> 24.8 us
    pallas_call x1, Pallas kernels: 27.1 us -> 24.8 us  [per_device(): pl.pallas_call(partial(kernel, levels, counts), out_shape=jax.ShapeDtypeS...]
where the time goes in v3:
time: 27.3 us; the launch traced here: 27.1 us
  Pallas kernels  24.8 us (91%)
  local copies, waits for them, and re-layouts  2.27 us (8%)
    pallas_call x1, Pallas kernels, per_device(): pl.pallas_call(partial(kernel, levels, counts), out_shape=jax.ShapeDtypeS...  24.8 us
    unnamed x3, local copies, waits for them, and re-layouts  2.27 us

profile of v3, /device:TPU:1, one launch (start us, length us, event | category | flops | bytes accessed | tf_op | source)
XLA Modules:
  0.0 27.1 jit_solution(3684736629481794636)
XLA Ops:
  0.0 0.0 copy-start
  0.0 0.9 %copy-done = f32[16,32,32]{2,1,0:T(8,128)S(1)} copy-done((f32[16,32,32]{2,1,0:T(8,128)S(1)}, f32[16,32,32]{2,1,0:T(8,128)}, u32[]{:S(2)}) %copy-start) | copy-done | bytes 65560
  1.0 24.8 %wavelet.1 = f32[4096,128]{1,0:T(8,128)S(1)} custom-call(f32[2048,256]{1,0:T(8,128)} %bitcast.7, f32[16,32,32]{2,1,0:T(8,128)S(1)} %copy-done), custom_call_target="tpu_custom_call" | custom-call | tf_op jit(solution)/shard_map/wavelet/pallas_call | solution.py:624
  25.8 1.3 %copy.4 = f32[2,32,32,256]{3,2,1,0:T(8,128)} copy(f32[2,32,32,256]{3,2,1,0:T(8,128)S(1)} %bitcast.6) | data formatting | bytes 4194304
Async XLA Ops:
  0.0 0.9 %copy-start = (f32[16,32,32]{2,1,0:T(8,128)S(1)}, f32[16,32,32]{2,1,0:T(8,128)}, u32[]{:S(2)}) copy-start(f32[16,32,32]{2,1,0:T(8,128)} %w_hbm.1) | copy-start | bytes 196612

commit v4 on v3

--- a/solution.py
+++ b/solution.py
@@ -110,14 +110,23 @@
             "gy": lax.rem(gy + dy + count_y, count_y),
         }
 
+    def exists(dx, dy):
+        x, y = gx + dx, gy + dy
+        inside_x = jnp.logical_and(x >= 0, x < count_x)
+        return jnp.logical_and(inside_x, jnp.logical_and(y >= 0, y < count_y))
+
     friends = [
         (dx, dy) for dx in (-2, -1, 0, 1, 2) for dy in (-1, 0, 1) if (dx, dy) != (0, 0)
     ]
     barrier = pltpu.get_barrier_semaphore()
     for dx, dy in friends:
-        pl.semaphore_signal(
-            barrier, inc=1, device_id=at(dx, dy), device_id_type=pl.DeviceIdType.MESH
-        )
+
+        @pl.when(exists(dx, dy))
+        def _():
+            pl.semaphore_signal(
+                barrier, inc=1, device_id=at(dx, dy), device_id_type=pl.DeviceIdType.MESH
+            )
+
     w_load = pltpu.make_async_copy(w_hbm, w_ref, in_sem.at[2])
     loads = [
         pltpu.make_async_copy(
@@ -217,11 +226,6 @@
             )
             ways.setdefault(way, []).append(copy)
         return ways
-
-    def exists(dx, dy):
-        x, y = gx + dx, gy + dy
-        inside_x = jnp.logical_and(x >= 0, x < count_x)
-        return jnp.logical_and(inside_x, jnp.logical_and(y >= 0, y < count_y))
 
     def start(ways, wanted):
         for way, group in ways.items():
@@ -547,7 +551,8 @@
         for j in range(3):
             take(3 + 3 * i + j)
 
-    pl.semaphore_wait(barrier, len(friends))
+    peers = sum(jnp.where(exists(dx, dy), 1, 0) for dx, dy in friends)
+    pl.semaphore_wait(barrier, peers)
     send_first()
 
     for k in range(LEVELS):

time: 27.3 us -> 25.7 us (0.941)
  the two profiles are of different devices: /device:TPU:1 before, /device:TPU:7 now
where the time goes in v4:
time: 25.7 us; the launch traced here: 25.5 us
  Pallas kernels  23.2 us (90%)
  local copies, waits for them, and re-layouts  2.27 us (9%)
    pallas_call x1, Pallas kernels, per_device(): pl.pallas_call(partial(kernel, levels, counts), out_shape=jax.ShapeDtypeS...  23.2 us
    unnamed x3, local copies, waits for them, and re-layouts  2.27 us

profile of v4, /device:TPU:7, one launch (start us, length us, event | category | flops | bytes accessed | tf_op | source)
XLA Modules:
  0.0 25.5 jit_solution(3765124210114064275)
XLA Ops:
  0.0 0.0 copy-start
  0.0 0.9 %copy-done = f32[16,32,32]{2,1,0:T(8,128)S(1)} copy-done((f32[16,32,32]{2,1,0:T(8,128)S(1)}, f32[16,32,32]{2,1,0:T(8,128)}, u32[]{:S(2)}) %copy-start) | copy-done | bytes 65560
  1.0 23.2 %wavelet.1 = f32[4096,128]{1,0:T(8,128)S(1)} custom-call(f32[2048,256]{1,0:T(8,128)} %bitcast.7, f32[16,32,32]{2,1,0:T(8,128)S(1)} %copy-done), custom_call_target="tpu_custom_call" | custom-call | tf_op jit(solution)/shard_map/wavelet/pallas_call | solution.py:629
  24.2 1.3 %copy.4 = f32[2,32,32,256]{3,2,1,0:T(8,128)} copy(f32[2,32,32,256]{3,2,1,0:T(8,128)S(1)} %bitcast.6) | data formatting | bytes 4194304
Async XLA Ops:
  0.0 0.9 %copy-start = (f32[16,32,32]{2,1,0:T(8,128)S(1)}, f32[16,32,32]{2,1,0:T(8,128)}, u32[]{:S(2)}) copy-start(f32[16,32,32]{2,1,0:T(8,128)} %w_hbm.1) | copy-start | bytes 196612
